TPU v7x, 256 devices: a whole 4x4x8 slice. The times are simulated.
256 devices in a mesh: seq: 16 (over z, core), tp: 16 (over y, x).
Axes of the slice: x: 4, y: 4, z: 8, core: 2. Of those that a mesh axis runs over, the one named last changes fastest.
Arguments:
- tokens: bfloat16 [8192, 4096], P('seq', 'tp'), may hold values from -60 to 60
- w_qkv: bfloat16 [4096, 3, 4096], P(None, None, 'tp'), may hold values from -0.09375 to 0.09375
- w_out: bfloat16 [4096, 4096], P('tp'), may hold values from -0.09375 to 0.09375
- rand_blocks: int32 [128, 32, 3], P('seq', 'tp'), may hold values from 0 to 127, as said below
- glob_blocks: int32 [2], replicated, may hold values from 0 to 127, as said below
- window_radius: int32 [32], P('tp'), may hold values from 0 to 1, as said below
Outputs:
- mixed: bfloat16 [8192, 4096], P('seq', 'tp')
Inputs may be any that keep to these rules, and one draw needn't show every extreme that they name: `rand_blocks`: split the blocks into aligned runs of 8 blocks. For one head and the query blocks of one run, the 24 entries lie at most C = ceil(8 * 3 / 16) times in any one run, and exactly C times in some run. `glob_blocks`: the 2 ids are distinct; the last block, 127, is always one of them. `window_radius`: some head has radius 1.
All inputs are finite; a program needn't handle non-finite values.
Results may differ from a plain program's by a relative error of at most 0.033.
Values may be sent and summed in bfloat16 or wider, within the bound.
No kernel may reach another device: no remote copies, remote signals or barrier semaphores. Data moves between devices by JAX's collectives and lax.ppermute only.
A program may use at most 128 MiB of HBM per device.

v0:
```python
import math
import jax
import jax.numpy as jnp
from jax import lax
from jax.sharding import PartitionSpec as P

DH = 128
BLK = 64
big_negative = -1e30


def padded_2(block, sides, width):
    for axis, dim in sides:
        count = lax.axis_size(axis)
        forward = [(i, i + 1) for i in range(count - 1)]
        backward = [(target, source) for source, target in forward]
        low = lax.ppermute(
            lax.slice_in_dim(block, block.shape[dim] - width, None, axis=dim), axis, forward
        )
        high = lax.ppermute(lax.slice_in_dim(block, 0, width, axis=dim), axis, backward)
        block = jnp.concatenate([low, block, high], axis=dim)
    return block


def body(tokens, w_qkv, w_out, rand_blocks, glob_blocks, window_radius):
    tok_rows = tokens.shape[0]
    local_blocks = tok_rows // BLK
    head_cols = w_qkv.shape[2]
    local_heads = head_cols // DH
    shard_count = lax.axis_size("seq")
    total_blocks = local_blocks * shard_count
    glob_count = glob_blocks.shape[0]
    scale = 1.0 / math.sqrt(DH)
    projected = jnp.einsum(
        "tf,fcj->ctj",
        lax.all_gather(tokens, "tp", axis=1, tiled=True),
        w_qkv,
        preferred_element_type=jnp.float32,
    )
    projected = projected.astype(jnp.bfloat16)
    query = projected[0].reshape(local_blocks, BLK, local_heads, DH)
    key_value = projected[1:]
    padded = padded_2(key_value, (("seq", 1),), BLK)
    padded_blocks = padded.reshape(2, local_blocks + 2, BLK, local_heads, DH)
    nearby = jnp.stack(
        [padded_blocks[:, offset : offset + local_blocks] for offset in range(3)], axis=2
    )
    my_shard = lax.axis_index("seq")
    first_block = my_shard * local_blocks
    block_ids = first_block + jnp.arange(local_blocks, dtype=jnp.int32)
    offsets = jnp.arange(3, dtype=jnp.int32) - 1
    targets = block_ids[:, None] + offsets[None, :]
    in_range = (targets >= 0) & (targets < total_blocks)
    near_valid = in_range[:, None, :] & (
        jnp.abs(offsets)[None, None, :] <= window_radius[None, :, None]
    )
    scores = (
        jnp.einsum("nqhd,nwkhd->nhqwk", query, nearby[0], preferred_element_type=jnp.float32)
        * scale
    )
    scores = jnp.where(near_valid[:, :, None, :, None], scores, big_negative)
    row_max = jnp.max(scores, axis=(3, 4))
    weights = jnp.exp(scores - row_max[..., None, None])
    row_sum = jnp.sum(weights, axis=(3, 4))
    accum = jnp.einsum(
        "nhqwk,nwkhd->nhqd",
        weights.astype(jnp.bfloat16),
        nearby[1],
        preferred_element_type=jnp.float32,
    )
    listed = jnp.concatenate(
        [
            rand_blocks,
            jnp.broadcast_to(glob_blocks[None, None, :], (local_blocks, local_heads, glob_count)),
        ],
        axis=2,
    )
    glob_local = glob_blocks - first_block
    glob_clip = jnp.clip(glob_local, 0, local_blocks - 1)
    glob_query = query[glob_clip]
    head_index = jnp.arange(local_heads, dtype=jnp.int32)[None, :, None]
    gathered = lax.all_gather(key_value, "seq", axis=1, tiled=True)
    list_sum = row_sum
    list_acc = accum
    dense_max = jnp.full((glob_count, local_heads, BLK), big_negative, jnp.float32)
    piece_rows = gathered.shape[1]
    piece_blocks = piece_rows // BLK
    key_blocks = gathered.reshape(2, piece_blocks, BLK, local_heads, DH)
    relative = listed - 0 // BLK
    inside = (relative >= 0) & (relative < piece_blocks)
    clipped = jnp.clip(relative, 0, piece_blocks - 1)
    keys_taken = key_blocks[0][clipped, :, head_index, :]
    values_taken = key_blocks[1][clipped, :, head_index, :]
    chosen = (
        jnp.einsum("nqhd,nhskd->nhqsk", query, keys_taken, preferred_element_type=jnp.float32)
        * scale
    )
    chosen = jnp.where(inside[:, :, None, :, None], chosen, big_negative)
    new_max = jnp.maximum(row_max, jnp.max(chosen, axis=(3, 4)))
    factor = jnp.exp(row_max - new_max)
    probs = jnp.exp(chosen - new_max[..., None, None])
    list_sum = list_sum * factor + jnp.sum(probs, axis=(3, 4))
    list_acc = list_acc * factor[..., None] + jnp.einsum(
        "nhqsk,nhskd->nhqd",
        probs.astype(jnp.bfloat16),
        values_taken,
        preferred_element_type=jnp.float32,
    )
    flat_keys = gathered[0].reshape(piece_rows, local_heads, DH)
    flat_values = gathered[1].reshape(piece_rows, local_heads, DH)
    dense = (
        jnp.einsum("gqhd,khd->ghqk", glob_query, flat_keys, preferred_element_type=jnp.float32)
        * scale
    )
    dense_new = jnp.maximum(dense_max, jnp.max(dense, axis=3))
    dense_probs = jnp.exp(dense - dense_new[..., None])
    dense_sum = jnp.sum(dense_probs, axis=3)
    dense_acc = jnp.einsum(
        "ghqk,khd->ghqd",
        dense_probs.astype(jnp.bfloat16),
        flat_values,
        preferred_element_type=jnp.float32,
    )
    attended = list_acc / list_sum[..., None]
    dense_out = dense_acc / dense_sum[..., None]
    for which in range(glob_count):
        owned_block = (block_ids == glob_blocks[which])[:, None, None, None]
        attended = jnp.where(owned_block, dense_out[which][None], attended)
    attended = attended.astype(jnp.bfloat16).transpose(0, 2, 1, 3).reshape(tok_rows, head_cols)
    partial_terms = jnp.dot(attended, w_out, preferred_element_type=jnp.float32)
    return lax.psum_scatter(
        partial_terms.astype(jnp.bfloat16), "tp", scatter_dimension=1, tiled=True
    )


def solution(mesh):
    return jax.shard_map(
        body,
        mesh=mesh,
        in_specs=(
            P("seq", "tp"),
            P(None, None, "tp"),
            P("tp", None),
            P("seq", "tp", None),
            P(),
            P("tp"),
        ),
        out_specs=P("seq", "tp"),
        check_vma=False,
    )
```

profile of v0, /device:TPU:2, one launch (start us, length us, event | category | flops | bytes accessed | tf_op | source)
XLA Modules:
  0.0 310.6 jit_solution(3259309802515597309)
XLA Ops:
  7.3 67.7 %all-gather.3.cloned.1.call-done = bf16[512,4096]{1,0:T(8,128)(2,1)} async-done(((bf16[512,256]{1,0:T(8,128)(2,1)}), bf16[512,4096]{1,0:T(8,128)(2,1)}) %all-gather.3.cloned.1.call-update) | async-done | bytes 4194320 | tf_op jit(solution)/shard_map/all_gather | solution.py:36
  75.0 7.5 %fusion.22 = bf16[3,512,256]{1,2,0:T(8,128)(2,1)S(1)} fusion(bf16[4096,3,256]{2,0,1:T(8,128)(2,1)} %param.7, bf16[512,4096]{1,0:T(8,128)(2,1)} %all-gather.3.cloned.1.call-done), kind=kOutput, calls=%fused_computation.29 | convolution fusion | flops 3221618688 | bytes 11272192 | tf_op jit(solution)/shard_map/tf,fcj->ctj/dot_general | solution.py:34
  82.5 1.0 copy-done.8
  83.5 0.8 slice.72
  85.8 1.7 fusion.76
  87.5 1.9 collective-permute-start
  89.4 1.3 collective-permute-start.1
  90.7 1.9 broadcast_compare_fusion.1
  92.6 1.0 slice.74
  95.0 1.4 pad_maximum_fusion.1
  96.4 1.2 copy.27
  97.6 1.9 reshape.176
  99.4 1.2 fusion.77
  103.2 36.9 %all-gather.5.cloned.1.call-done = bf16[2,8192,256]{1,2,0:T(8,128)(2,1)} async-done(((bf16[2,512,256]{1,2,0:T(8,128)(2,1)}), bf16[2,8192,256]{1,2,0:T(8,128)(2,1)}) %all-gather.5.cloned.1.call-update) | async-done | bytes 8388624 | tf_op jit(solution)/shard_map/all_gather | solution.py:82
  140.1 5.9 %fusion.75 = (bf16[1,8192,256]{1,2,0:T(8,128)(2,1)}, bf16[1,8192,256]{1,2,0:T(8,128)(2,1)}) fusion(bf16[2,8192,256]{1,2,0:T(8,128)(2,1)} %all-gather.5.cloned.1.call-done), kind=kLoop, calls=%fused_computation.87 | loop fusion | bytes 16777216 | tf_op jit(solution)/shard_map/slice | solution.py:110
  146.1 12.6 %reshape.208 = bf16[128,64,2,128]{1,0,3,2:T(8,128)(2,1)} reshape(bf16[1,8192,256]{1,2,0:T(8,128)(2,1)} %get-tuple-element.8) | data formatting | bytes 8388608 | tf_op jit(solution)/shard_map/squeeze | solution.py:92
  158.7 3.4 %fusion.79 = f32[2,8192,128]{1,2,0:S(1)} fusion(bf16[2,128,128]{1,2,0:T(8,128)(2,1)S(1)} %bitcast.134, bf16[8192,2,128]{0,2,1:T(8,128)(2,1)} %bitcast.123), kind=kOutput, calls=%fused_computation.91 | convolution fusion | flops 536870912 | bytes 12648448
  162.1 0.8 bitcast_reduce_fusion
  162.9 2.4 copy-done.1
  165.3 1.5 fusion.1
  166.9 12.6 %reshape.209 = bf16[128,64,2,128]{1,0,3,2:T(8,128)(2,1)} reshape(bf16[1,8192,256]{1,2,0:T(8,128)(2,1)} %get-tuple-element.7) | data formatting | bytes 8388608 | tf_op jit(solution)/shard_map/squeeze | solution.py:93
  179.4 6.3 %fusion.49 = bf16[2,2,64,128]{3,2,0,1:T(8,128)(2,1)S(1)} fusion(bf16[8192,2,128,1]{0,2,3,1:T(8,128)(2,1)} %bitcast.124, f32[2,8192,2,64]{1,3,2,0:T(8,128)} %bitcast.122, f32[2,2,64]{2,0,1:T(2,128)S(1)} %broadcast_maximum_fusion, f32[2,2,64]{2,0,1:T(2,128)S(1)} %fusion.1), kind=kOutput, calls=%fused_computation.41 | convolution fusion | flops 543227904 | bytes 12650496 | tf_op jit(solution)/shard_map/ghqk,khd->ghqd/dot_general | solution.py:118
  185.7 10.5 %copy.39 = bf16[128,64,2,128]{3,1,2,0:T(8,128)(2,1)} copy(bf16[128,64,2,128]{1,0,3,2:T(8,128)(2,1)} %reshape.209) | data formatting | bytes 8388608 | tf_op jit(solution)/shard_map/squeeze | solution.py:93
  196.2 10.5 %copy.36 = bf16[128,64,2,128]{3,1,2,0:T(8,128)(2,1)} copy(bf16[128,64,2,128]{1,0,3,2:T(8,128)(2,1)} %reshape.208) | data formatting | bytes 8388608 | tf_op jit(solution)/shard_map/squeeze | solution.py:92
  206.7 4.5 %gather_fusion.2 = bf16[80,64,128]{2,1,0:T(8,128)(2,1)} fusion(bf16[128,64,2,128]{3,1,2,0:T(8,128)(2,1)} %copy.39, s32[80]{0:T(128)S(1)} %reshape.186), kind=kCustom, calls=%fused_computation.2 | custom fusion | bytes 2622080 | tf_op jit(solution)/shard_map/gather | solution.py:93
  211.2 3.4 %gather_fusion.1 = bf16[80,64,128]{2,1,0:T(8,128)(2,1)S(1)} fusion(bf16[128,64,2,128]{3,1,2,0:T(8,128)(2,1)} %copy.36, s32[80]{0:T(128)S(1)} %reshape.186), kind=kCustom, calls=%fused_computation.1 | custom fusion | bytes 2622080 | tf_op jit(solution)/shard_map/gather | solution.py:92
  214.6 1.7 fusion.9
  216.4 0.8 fusion.10
  217.2 1.0 fusion.31
  218.2 1.2 fusion.46
  219.8 3.2 %convolution_convert_fusion = bf16[512,4096]{1,0:T(8,128)(2,1)} fusion(bf16[256,4096]{1,0:T(8,128)(2,1)S(1)} %copy-done, bf16[64,8,2,128]{3,2,1,0:T(2,128)(2,1)S(1)} %bitcast.133), kind=kOutput, calls=%fused_computation.8 | convolution fusion | flops 1075838976 | bytes 6553600 | tf_op jit(solution)/shard_map/dot_general | solution.py:130
  223.0 81.1 %reduce-scatter.2.cloned.1.call-done = bf16[512,256]{1,0:T(8,128)(2,1)} async-done(((bf16[512,4096]{1,0:T(8,128)(2,1)}), bf16[512,256]{1,0:T(8,128)(2,1)}) %reduce-scatter.2.cloned.1.call-update) | async-done | bytes 262160 | tf_op jit(solution)/shard_map/reduce_scatter | solution.py:131
  (70 shorter events, 6.5 us)
Async XLA Ops:
  6.5 213.2 %copy-start = (bf16[256,4096]{1,0:T(8,128)(2,1)S(1)}, bf16[256,4096]{1,0:T(8,128)(2,1)}, u32[]{:S(2)}) copy-start(bf16[256,4096]{1,0:T(8,128)(2,1)} %param.8) | copy-start | bytes 6291460
  6.5 68.5 %all-gather.3.cloned.1.call-start = ((), (), s32[]{:S(2)}) async-start(), calls=%async_computation.1 | async-start | bytes 4456448 | tf_op jit(solution)/shard_map/all_gather | solution.py:36
  7.3 77.1 %copy-start.12 = (s32[2]{0:T(128)S(1)}, s32[2]{0:T(128)}, u32[]{:S(2)}) copy-start(s32[2]{0:T(128)} %param.10) | copy-start | bytes 28
  7.3 77.2 %copy-start.11 = (s32[8,2,3]{0,1,2:T(2,128)S(1)}, s32[8,2,3]{0,1,2:T(2,128)}, u32[]{:S(2)}) copy-start(s32[8,2,3]{0,1,2:T(2,128)} %param.9) | copy-start | bytes 580
  7.3 78.3 %copy-start.15 = (s32[2]{0:T(128)S(1)}, s32[2]{0:T(128)}, u32[]{:S(2)}) copy-start(s32[2]{0:T(128)} %param.11) | copy-start | bytes 28
  7.3 132.8 %all-gather.5.cloned.1.call-start = ((), (), s32[]{:S(2)}) async-start(), calls=%async_computation.2 | async-start | bytes 8912896 | tf_op jit(solution)/shard_map/all_gather | solution.py:82
  82.5 1.0 copy-start.8
  84.3 10.7 %copy-start.4 = (bf16[2,512,256]{1,2,0:T(8,128)(2,1)S(1)}, bf16[2,512,256]{1,2,0:T(8,128)(2,1)}, u32[]{:S(2)}) copy-start(bf16[2,512,256]{1,2,0:T(8,128)(2,1)} %slice.72) | copy-start | bytes 1572868
  84.3 219.8 %reduce-scatter.2.cloned.1.call-start = ((), (), s32[]{:S(2)}) async-start(), calls=%async_computation.3 | async-start | bytes 4456448 | tf_op jit(solution)/shard_map/reduce_scatter | solution.py:131
  87.5 7.5 %collective-permute-start = (bf16[2,64,256]{1,2,0:T(8,128)(2,1)}, bf16[2,64,256]{1,2,0:T(8,128)(2,1)}, u32[]{:S(2)}, u32[]{:S(2)}) collective-permute-start(bf16[2,64,256]{1,2,0:T(8,128)(2,1)} %get-tuple-element.9), channel_id=1, source_target_pairs={{0,16},{16,32},{32,48},{48,64},{64,80},{80,96},{96,112},{112,128},... | collective-permute-start | bytes 196616 | tf_op jit(solution)/shard_map/ppermute | solution.py:17
  89.4 5.6 %collective-permute-start.1 = (bf16[2,64,256]{1,2,0:T(8,128)(2,1)S(1)}, bf16[2,64,256]{1,2,0:T(8,128)(2,1)}, u32[]{:S(2)}, u32[]{:S(2)}) collective-permute-start(bf16[2,64,256]{1,2,0:T(8,128)(2,1)S(1)} %get-tuple-element.10), channel_id=1, source_target_pairs={{16,0},{32,16},{48,32},{64,48},{80,64},{96,80},{112,96},{128,112},... | collective-permute-start | bytes 196616 | tf_op jit(solution)/shard_map/ppermute | solution.py:20
  93.8 7.4 %copy-start.5 = (bf16[8,64,2,128]{3,2,1,0:T(2,128)(2,1)}, bf16[8,64,2,128]{3,2,1,0:T(2,128)(2,1)S(1)}, u32[]{:S(2)}) copy-start(bf16[8,64,2,128]{3,2,1,0:T(2,128)(2,1)S(1)} %reshape_squeeze.11) | copy-start | bytes 786436
  101.1 1.2 copy-start.6
  101.5 1.2 copy-start.2
  146.1 12.6 %copy-start.10 = (bf16[2,64,2,128]{3,1,0,2:T(8,128)(2,1)S(1)}, bf16[2,64,2,128]{3,1,0,2:T(8,128)(2,1)}, u32[]{:S(2)}) copy-start(bf16[2,64,2,128]{3,1,0,2:T(8,128)(2,1)} %copy.25) | copy-start | bytes 196612
  162.1 3.2 %copy-start.1 = (f32[2,8192,128]{1,2,0}, f32[2,8192,128]{1,2,0:S(1)}, u32[]{:S(2)}) copy-start(f32[2,8192,128]{1,2,0:S(1)} %fusion.79) | copy-start | bytes 25165828
  214.6 2.6 copy-start.3
  214.6 2.6 copy-start.7
  216.4 1.8 copy-start.9
  216.4 1.8 copy-start.13
  216.4 1.8 copy-start.14
Sparse Core Ops, SparseCore 0:
  9.8 65.2 all-gather.2
  84.4 55.6 all-gather.4
  223.1 80.8 reduce-scatter.1
where the time goes:
time: 312 us; the launch traced here: 311 us
  waiting for transfers between devices  186 us (60%)
  local copies, waits for them, and re-layouts  75 us (24%)
  matrix products  24.7 us (8%)
  between operations  13.5 us (4%)
  other arithmetic  7.69 us (2%)
  starting transfers between devices  3.3 us (1%)
    reduce_scatter x1, waiting for transfers between devices, body(): lax.psum_scatter(partial_terms.astype(jnp.bfloat16), 'tp', scatter_dimens...  81.1 us
    all_gather x1, waiting for transfers between devices, body(): lax.all_gather(tokens, 'tp', axis=1, tiled=True)  67.7 us
    all_gather x1, waiting for transfers between devices, body(): gathered = lax.all_gather(key_value, 'seq', axis=1, tiled=True)  36.9 us
    squeeze x2, local copies, waits for them, and re-layouts, body(): keys_taken = key_blocks[0][clipped, :, head_index, :]  23.1 us
    squeeze x2, local copies, waits for them, and re-layouts, body(): values_taken = key_blocks[1][clipped, :, head_index, :]  23 us
    dot_general x1, matrix products, body(): jnp.einsum('tf,fcj->ctj', lax.all_gather(tokens, 'tp', axis=1, tiled=True...  7.46 us
    dot_general x1, matrix products, body(): jnp.einsum('ghqk,khd->ghqd', dense_probs.astype(jnp.bfloat16), flat_value...  6.28 us
  transfers between devices with their start and end apart: 5, of which 3 were waited for; matrix products, arithmetic and copies ran while one was open for 5% of the time, Pallas kernels for 0%

commit v1 on v0

--- a/solution.py
+++ b/solution.py
@@ -7,6 +7,13 @@
 DH = 128
 BLK = 64
 big_negative = -1e30
+
+
+def exchange_gather(block, mesh_axis, dim):
+    size = lax.axis_size(mesh_axis)
+    blocks = jnp.stack([block for _ in range(size)])
+    blocks = lax.all_to_all(blocks, mesh_axis, split_axis=0, concat_axis=0)
+    return jnp.concatenate(blocks, axis=dim)
 
 
 def padded_2(block, sides, width):
@@ -79,7 +86,7 @@
     glob_clip = jnp.clip(glob_local, 0, local_blocks - 1)
     glob_query = query[glob_clip]
     head_index = jnp.arange(local_heads, dtype=jnp.int32)[None, :, None]
-    gathered = lax.all_gather(key_value, "seq", axis=1, tiled=True)
+    gathered = exchange_gather(key_value, "seq", 1)
     list_sum = row_sum
     list_acc = accum
     dense_max = jnp.full((glob_count, local_heads, BLK), big_negative, jnp.float32)

time: 312 us -> 446 us (1.43)
  waiting for transfers between devices: 186 us -> 324 us
  starting transfers between devices: 3.3 us -> 11.6 us
  local copies, waits for them, and re-layouts: 75 us -> 67.3 us
    all_to_all x0 -> x1, waiting for transfers between devices: none -> 164 us  [exchange_gather(): blocks = lax.all_to_all(blocks, mesh_axis, split_axis=0, concat_axis=0)]
    all_gather x1 -> x0, waiting for transfers between devices: 36.9 us -> none  [body(): gathered = lax.all_gather(key_value, 'seq', axis=1, tiled=True)]
    another operation x0 -> x3, local copies, waits for them, and re-layouts: none -> 18 us  [the longest x1 6.92 us: body(): flat_keys = gathered[0].reshape(piece_rows, local_heads, DH)]
    squeeze x2, local copies, waits for them, and re-layouts: 23 us -> 10.2 us  [body(): values_taken = key_blocks[1][clipped, :, head_index, :]]
    reduce_scatter x1, waiting for transfers between devices: 81.1 us -> 91.8 us  [body(): lax.psum_scatter(partial_terms.astype(jnp.bfloat16), 'tp', scatter_dimens...]
    squeeze x2, local copies, waits for them, and re-layouts: 23.1 us -> 12.3 us  [body(): keys_taken = key_blocks[0][clipped, :, head_index, :]]
    all_to_all x0 -> x1, starting transfers between devices: none -> 7.31 us  [exchange_gather(): blocks = lax.all_to_all(blocks, mesh_axis, split_axis=0, concat_axis=0)]
  transfers between devices with their start and end apart: 5 -> 5, of which waited for: 3 -> 3; matrix products, arithmetic and copies ran while one was open for 5% -> 3% of each run, Pallas kernels for 0% -> 0%
where the time goes in v1:
time: 446 us; the launch traced here: 445 us
  waiting for transfers between devices  324 us (73%)
  local copies, waits for them, and re-layouts  67.3 us (15%)
  matrix products  20.8 us (5%)
  between operations  13.8 us (3%)
  starting transfers between devices  11.6 us (3%)
  other arithmetic  7.91 us (2%)
    all_to_all x1, waiting for transfers between devices, exchange_gather(): blocks = lax.all_to_all(blocks, mesh_axis, split_axis=0, concat_axis=0)  164 us
    reduce_scatter x1, waiting for transfers between devices, body(): lax.psum_scatter(partial_terms.astype(jnp.bfloat16), 'tp', scatter_dimens...  91.8 us
    all_gather x1, waiting for transfers between devices, body(): lax.all_gather(tokens, 'tp', axis=1, tiled=True)  67.8 us
    squeeze x2, local copies, waits for them, and re-layouts, body(): keys_taken = key_blocks[0][clipped, :, head_index, :]  12.3 us
    squeeze x2, local copies, waits for them, and re-layouts, body(): values_taken = key_blocks[1][clipped, :, head_index, :]  10.2 us
  transfers between devices with their start and end apart: 5, of which 3 were waited for; matrix products, arithmetic and copies ran while one was open for 3% of the time, Pallas kernels for 0%

profile of v1, /device:TPU:2, one launch (start us, length us, event | category | flops | bytes accessed | tf_op | source)
XLA Modules:
  0.0 445.2 jit_solution(1886742238132062184)
XLA Ops:
  7.3 67.8 %all-gather.2.cloned.1.call-done = bf16[512,4096]{1,0:T(8,128)(2,1)} async-done(((bf16[512,256]{1,0:T(8,128)(2,1)}), bf16[512,4096]{1,0:T(8,128)(2,1)}) %all-gather.2.cloned.1.call-update) | async-done | bytes 4194320 | tf_op jit(solution)/shard_map/all_gather | solution.py:43
  75.0 7.5 %fusion.25 = bf16[3,512,256]{1,2,0:T(8,128)(2,1)S(1)} fusion(bf16[4096,3,256]{2,0,1:T(8,128)(2,1)} %param.7, bf16[512,4096]{1,0:T(8,128)(2,1)} %all-gather.2.cloned.1.call-done), kind=kOutput, calls=%fused_computation.32 | convolution fusion | flops 3221618688 | bytes 11272192 | tf_op jit(solution)/shard_map/tf,fcj->ctj/dot_general | solution.py:41
  82.5 0.9 copy-done.10
  83.6 4.2 stack.10
  87.8 7.3 %all-to-all-start = ((bf16[16,2,512,256]{3,2,1,0:T(8,128)(2,1)}), bf16[16,2,512,256]{3,2,1,0:T(8,128)(2,1)}, u32[]{:S(2)}, u32[]{:S(2)}) async-start(bf16[16,2,512,256]{3,2,1,0:T(8,128)(2,1)} %stack.10), calls=%async_computation | async-start | bytes 16777216 | tf_op jit(solution)/shard_map/all_to_all | solution.py:15
  97.3 2.9 collective-permute-start
  100.2 1.3 collective-permute-start.1
  101.5 1.3 broadcast_compare_fusion.1
  103.5 1.1 copy.61
  105.4 2.2 pad_maximum_fusion.1
  107.6 2.2 copy.66
  109.7 1.9 reshape.186
  111.6 1.5 fusion.84
  115.9 163.5 %all-to-all-done = bf16[16,2,512,256]{3,2,1,0:T(8,128)(2,1)} async-done(((bf16[16,2,512,256]{3,2,1,0:T(8,128)(2,1)}), bf16[16,2,512,256]{3,2,1,0:T(8,128)(2,1)}, u32[]{:S(2)}, u32[]{:S(2)}) %all-to-all-start) | async-done | bytes 8388640 | tf_op jit(solution)/shard_map/all_to_all | solution.py:15
  279.4 5.8 %fusion.82 = (bf16[1,16,512,256]{3,2,0,1:T(8,128)(2,1)}, bf16[1,16,512,256]{3,2,0,1:T(8,128)(2,1)}) fusion(bf16[2,16,512,256]{3,2,0,1:T(8,128)(2,1)} %bitcast.3), kind=kLoop, calls=%fused_computation.90 | loop fusion | bytes 16777216 | tf_op jit(solution)/shard_map/slice | solution.py:117
  285.2 6.9 %squeeze.22 = bf16[128,64,2,128]{3,2,1,0:T(2,128)(2,1)} reshape(bf16[1,16,512,256]{3,2,0,1:T(8,128)(2,1)} %get-tuple-element.8) | data formatting | bytes 8388608 | tf_op jit(solution)/shard_map/squeeze | solution.py:99
  292.1 6.9 %reshape.219 = bf16[8192,2,128]{2,1,0:T(2,128)(2,1)} reshape(bf16[1,16,512,256]{3,2,0,1:T(8,128)(2,1)} %get-tuple-element.8) | data formatting | bytes 8388608 | tf_op jit(solution)/shard_map/reshape;squeeze | solution.py:116
  299.0 6.9 %reshape.218 = bf16[8192,2,128]{2,1,0:T(2,128)(2,1)} reshape(bf16[1,16,512,256]{3,2,0,1:T(8,128)(2,1)} %get-tuple-element.7) | data formatting | bytes 8388608 | tf_op jit(solution)/shard_map/reshape;squeeze | solution.py:117
  305.9 7.0 %squeeze.23 = bf16[128,64,2,128]{3,2,1,0:T(2,128)(2,1)} reshape(bf16[1,16,512,256]{3,2,0,1:T(8,128)(2,1)} %get-tuple-element.7) | data formatting | bytes 8388608 | tf_op jit(solution)/shard_map/squeeze | solution.py:100
  312.9 5.4 %copy.74 = bf16[128,64,2,128]{3,1,2,0:T(8,128)(2,1)} copy(bf16[128,64,2,128]{3,2,1,0:T(2,128)(2,1)} %squeeze.22) | data formatting | bytes 8388608 | tf_op jit(solution)/shard_map/squeeze | solution.py:99
  318.3 3.4 gather_fusion.1
  321.8 1.7 fusion.12
  324.3 1.6 fusion.34
  326.0 0.9 copy-done.1
  326.9 1.3 fusion.5
  328.9 1.5 fusion.1
  331.1 2.1 fusion.42
  333.3 3.2 copy.76
  336.5 3.4 gather_fusion.2
  340.0 3.0 fusion.56
  343.3 3.2 convolution_convert_fusion
  346.5 91.8 %reduce-scatter.2.cloned.1.call-done = bf16[512,256]{1,0:T(8,128)(2,1)} async-done(((bf16[512,4096]{1,0:T(8,128)(2,1)}), bf16[512,256]{1,0:T(8,128)(2,1)}) %reduce-scatter.2.cloned.1.call-update) | async-done | bytes 262160 | tf_op jit(solution)/shard_map/reduce_scatter | solution.py:138
  (71 shorter events, 9.8 us)
Async XLA Ops:
  6.5 336.7 %copy-start = (bf16[256,4096]{1,0:T(8,128)(2,1)S(1)}, bf16[256,4096]{1,0:T(8,128)(2,1)}, u32[]{:S(2)}) copy-start(bf16[256,4096]{1,0:T(8,128)(2,1)} %param.8) | copy-start | bytes 6291460
  6.5 68.5 %all-gather.2.cloned.1.call-start = ((), (), s32[]{:S(2)}) async-start(), calls=%async_computation.2 | async-start | bytes 4456448 | tf_op jit(solution)/shard_map/all_gather | solution.py:43
  82.5 0.9 copy-start.10
  87.8 7.4 %copy-start.13 = (s32[2]{0:T(128)S(1)}, s32[2]{0:T(128)}, u32[]{:S(2)}) copy-start(s32[2]{0:T(128)} %param.10) | copy-start | bytes 28
  87.8 7.5 %copy-start.12 = (s32[8,2,3]{0,1,2:T(2,128)S(1)}, s32[8,2,3]{0,1,2:T(2,128)}, u32[]{:S(2)}) copy-start(s32[8,2,3]{0,1,2:T(2,128)} %param.9) | copy-start | bytes 580
  87.8 8.6 %copy-start.14 = (s32[2]{0:T(128)S(1)}, s32[2]{0:T(128)}, u32[]{:S(2)}) copy-start(s32[2]{0:T(128)} %param.11) | copy-start | bytes 28
  87.8 8.7 %copy-start.11 = (bf16[3,512,256]{1,2,0:T(8,128)(2,1)S(1)}, bf16[3,512,256]{1,2,0:T(8,128)(2,1)}, u32[]{:S(2)}) copy-start(bf16[3,512,256]{1,2,0:T(8,128)(2,1)} %copy-done.10) | copy-start | bytes 2359300
  87.8 191.6 %all-to-all-start = ((bf16[16,2,512,256]{3,2,1,0:T(8,128)(2,1)}), bf16[16,2,512,256]{3,2,1,0:T(8,128)(2,1)}, u32[]{:S(2)}, u32[]{:S(2)}) async-start(bf16[16,2,512,256]{3,2,1,0:T(8,128)(2,1)} %stack.10), calls=%async_computation | async-start | bytes 16777216 | tf_op jit(solution)/shard_map/all_to_all | solution.py:15
  95.1 343.2 %reduce-scatter.2.cloned.1.call-start = ((), (), s32[]{:S(2)}) async-start(), calls=%async_computation.3 | async-start | bytes 4456448 | tf_op jit(solution)/shard_map/reduce_scatter | solution.py:138
  97.3 8.0 %collective-permute-start = (bf16[2,64,256]{1,2,0:T(8,128)(2,1)}, bf16[2,64,256]{1,2,0:T(8,128)(2,1)}, u32[]{:S(2)}, u32[]{:S(2)}) collective-permute-start(bf16[2,64,256]{1,2,0:T(8,128)(2,1)} %get-tuple-element.9), channel_id=1, source_target_pairs={{0,16},{16,32},{32,48},{48,64},{64,80},{80,96},{96,112},{112,128},... | collective-permute-start | bytes 196616 | tf_op jit(solution)/shard_map/ppermute | solution.py:24
  100.2 5.1 %collective-permute-start.1 = (bf16[2,64,256]{1,2,0:T(8,128)(2,1)}, bf16[2,64,256]{1,2,0:T(8,128)(2,1)}, u32[]{:S(2)}, u32[]{:S(2)}) collective-permute-start(bf16[2,64,256]{1,2,0:T(8,128)(2,1)} %get-tuple-element.10), channel_id=1, source_target_pairs={{16,0},{32,16},{48,32},{64,48},{80,64},{96,80},{112,96},{128,112},... | collective-permute-start | bytes 196616 | tf_op jit(solution)/shard_map/ppermute | solution.py:27
  104.7 9.1 %copy-start.7 = (bf16[8,64,2,128]{3,2,1,0:T(2,128)(2,1)}, bf16[8,64,2,128]{3,2,1,0:T(2,128)(2,1)S(1)}, u32[]{:S(2)}) copy-start(bf16[8,64,2,128]{3,2,1,0:T(2,128)(2,1)S(1)} %reshape_squeeze.11) | copy-start | bytes 786436
  113.7 1.2 copy-start.8
  114.2 1.2 copy-start.4
  321.8 2.6 copy-start.5
  321.8 2.6 copy-start.9
  323.5 2.5 copy-start.6
  323.5 3.4 copy-start.1
  328.9 2.2 copy-start.3
  331.1 2.2 copy-start.2
Sparse Core Ops, SparseCore 0:
  9.8 65.2 all-gather.1
  346.6 91.6 reduce-scatter.1
